TPU v7x, 256 devices: a whole 4x4x8 slice. The times are simulated.
256 devices in a mesh: dp: 32 (over y, x, core), filter: 8 (over z).
Axes of the slice: x: 4, y: 4, z: 8, core: 2. Of those that a mesh axis runs over, the one named last changes fastest.
Arguments:
- inputs: bfloat16 [32, 48, 24, 1024], P('dp', None, None, 'filter'), may hold values from -6 to 6
- kernel: bfloat16 [3, 3, 1024, 1024], P(None, None, 'filter'), may hold values from -0.0625 to 0.0625
- cotangent: bfloat16 [32, 48, 24, 1024], P('dp', 'filter'), may hold values from -6 to 6
Outputs:
- outputs: bfloat16 [32, 48, 24, 1024], P('dp', 'filter')
- input_grad: bfloat16 [32, 48, 24, 1024], P('dp', None, None, 'filter')
- kernel_grad: float32 [1024, 3, 3, 1024], P('dp', None, None, 'filter')
All inputs are finite; a program needn't handle non-finite values.
Results may differ from a plain program's by a relative error of at most 0.001.
Values may be sent and summed in bfloat16 or wider, within the bound.
No kernel may reach another device: no remote copies, remote signals or barrier semaphores. Data moves between devices by JAX's collectives and lax.ppermute only.
A program may use at most 128 MiB of HBM per device.

v0:
```python
import jax
import jax.numpy as jnp
from jax import lax
from jax.sharding import PartitionSpec as P


def conv_rows(xpad, weights, count, width):
    total = jnp.zeros((count, width, weights.shape[3]), jnp.float32)
    for a in range(3):
        for b in range(3):
            total = total + jnp.einsum(
                "hwi,io->hwo",
                xpad[a : a + count, b : b + width],
                weights[a, b],
                preferred_element_type=jnp.float32,
            )
    return total


def on_device(inputs, kernel, cotangent):
    sample = inputs[0]
    height = sample.shape[0]
    width = sample.shape[1]
    local_in = sample.shape[2]
    channels = kernel.shape[3]
    groups = lax.axis_size("filter")
    my_rows = height // groups
    xpad = jnp.pad(sample, ((1, 1), (1, 1), (0, 0)))
    summed = lax.psum_scatter(
        conv_rows(xpad, kernel, my_rows * lax.axis_size("filter"), width),
        "filter",
        scatter_dimension=0,
        tiled=True,
    )
    outputs = summed.astype(jnp.bfloat16)[None]
    start = jnp.int32(0)
    back_pad = jnp.zeros((height + 2, width + 2, local_in), jnp.float32)
    grad_rows = lax.all_gather(cotangent, "filter", axis=1, tiled=True)[0]
    count = grad_rows.shape[0]
    taps = []
    for a in range(3):
        for b in range(3):
            contrib = jnp.einsum(
                "hwo,io->hwi", grad_rows, kernel[a, b], preferred_element_type=jnp.float32
            )
            region = lax.dynamic_slice(back_pad, (start + a, b, 0), (count, width, local_in))
            back_pad = lax.dynamic_update_slice(back_pad, region + contrib, (start + a, b, 0))
            taps.append(
                jnp.einsum(
                    "hwi,hwo->oi",
                    xpad[a : a + count, b : b + width],
                    grad_rows,
                    preferred_element_type=jnp.float32,
                )
            )
    grads = jnp.stack(taps, 1).reshape(channels, 3, 3, local_in)
    back_pad, grads = (back_pad, grads)
    input_grad = back_pad[1:-1, 1:-1].astype(jnp.bfloat16)[None]
    samples = lax.axis_size("dp")
    scale = 1.0 / jnp.sqrt(jnp.float32(samples * height * width))
    whole = lax.psum(grads, "dp")
    share = channels // samples
    mine = lax.dynamic_slice_in_dim(whole, lax.axis_index("dp") * share, share, 0)
    return (outputs, input_grad, mine * scale)


def solution(mesh):
    return jax.shard_map(
        on_device,
        mesh=mesh,
        in_specs=(
            P("dp", None, None, "filter"),
            P(None, None, "filter", None),
            P("dp", "filter", None, None),
        ),
        out_specs=(
            P("dp", "filter", None, None),
            P("dp", None, None, "filter"),
            P("dp", None, None, "filter"),
        ),
        check_vma=False,
    )
```

profile of v0, /device:TPU:1, one launch (start us, length us, event | category | flops | bytes accessed | tf_op | source)
XLA Modules:
  0.0 268.3 jit_solution(1624768555959365311)
XLA Ops:
  7.2 0.0 all-gather.2.cloned.1.call-start
  7.2 0.7 all-gather.2.cloned.1.call-update
  7.9 0.0 all-reduce.4.cloned.1.call-start
  7.9 0.0 copy-start.1
  8.0 4.1 %fusion.124 = f32[48,24,1024]{2,1,0:T(8,128)} fusion(bf16[3,3,128,1024]{3,2,1,0:T(8,128)(2,1)} %param.4, bf16[48,24,128]{2,1,0:T(8,128)(2,1)} %bitcast.236), kind=kOutput, calls=%fused_computation.79 | convolution fusion | flops 301989888 | bytes 5275648 | tf_op jit(solution)/shard_map/hwi,io->hwo/dot_general | solution.py:11
  12.0 0.0 copy-done.1
  12.0 3.8 %fusion.127 = f32[48,24,1024]{2,1,0:T(8,128)} fusion(bf16[3,3,128,1024]{3,2,1,0:T(8,128)(2,1)} %param.4, bf16[48,24,128]{2,1,0:T(8,128)(2,1)S(1)} %bitcast.237), kind=kOutput, calls=%fused_computation.82 | convolution fusion | flops 301989888 | bytes 5275648 | tf_op jit(solution)/shard_map/hwi,io->hwo/dot_general | solution.py:11
  15.8 3.9 %fusion.130 = f32[48,24,1024]{2,1,0:T(8,128)} fusion(bf16[3,3,128,1024]{3,2,1,0:T(8,128)(2,1)} %param.4, bf16[48,24,128]{2,1,0:T(8,128)(2,1)S(1)} %bitcast.238), kind=kOutput, calls=%fused_computation.85 | convolution fusion | flops 301989888 | bytes 5275648 | tf_op jit(solution)/shard_map/hwi,io->hwo/dot_general | solution.py:11
  19.8 3.9 %fusion.136 = f32[48,24,1024]{2,1,0:T(8,128)} fusion(bf16[3,3,128,1024]{3,2,1,0:T(8,128)(2,1)} %param.4, bf16[48,24,128]{2,1,0:T(8,128)(2,1)S(1)} %bitcast.239), kind=kOutput, calls=%fused_computation.91 | convolution fusion | flops 301989888 | bytes 5275648 | tf_op jit(solution)/shard_map/hwi,io->hwo/dot_general | solution.py:11
  23.6 3.9 %fusion.139 = f32[48,24,1024]{2,1,0:T(8,128)} fusion(bf16[3,3,128,1024]{3,2,1,0:T(8,128)(2,1)} %param.4, bf16[48,24,128]{2,1,0:T(8,128)(2,1)S(1)} %bitcast.240), kind=kOutput, calls=%fused_computation.94 | convolution fusion | flops 301989888 | bytes 5275648 | tf_op jit(solution)/shard_map/hwi,io->hwo/dot_general | solution.py:11
  27.5 24.7 %all-gather.2.cloned.1.call-done = bf16[1,48,24,1024]{3,2,0,1:T(8,128)(2,1)} async-done(((bf16[1,6,24,1024]{3,2,0,1:T(8,128)(2,1)}), bf16[1,48,24,1024]{3,2,0,1:T(8,128)(2,1)}) %all-gather.2.cloned.1.call-update) | async-done | bytes 2359312 | tf_op jit(solution)/shard_map/all_gather | solution.py:38
  52.3 0.0 copy-start
  52.3 3.2 %fusion.69 = f32[1024,9,128]{0,2,1:T(8,128)} fusion(bf16[1,48,24,1024]{3,2,0,1:T(8,128)(2,1)} %all-gather.2.cloned.1.call-done, bf16[48,24,128]{2,1,0:T(8,128)(2,1)S(1)} %bitcast.241), kind=kOutput, calls=%fused_computation.48 | convolution fusion | flops 301989888 | bytes 3178496 | tf_op jit(solution)/shard_map/hwi,hwo->oi/dot_general | solution.py:49
  55.4 0.0 copy-done
  55.4 1.3 fusion.75
  56.8 1.4 fusion.81
  58.1 1.4 fusion.87
  59.5 1.4 fusion.93
  60.9 1.3 fusion.99
  62.2 1.3 fusion.105
  63.5 1.4 fusion.111
  64.9 1.4 fusion.117
  66.3 6.0 %copy.46 = f32[1024,3,3,128]{3,0,2,1:T(8,128)} copy(f32[1024,3,3,128]{0,3,2,1:T(8,128)} %bitcast.58) | data formatting | bytes 9437184 | tf_op jit(solution)/shard_map/reshape | solution.py:56
  72.3 0.0 all-reduce.4.cloned.1.call-update
  72.3 0.0 reduce-scatter.2.cloned.1.call-start
  72.4 0.0 slice-start
  72.4 0.0 slice-start.2
  72.4 4.2 %fusion.145 = f32[48,24,1024]{2,1,0:T(8,128)} fusion(bf16[3,3,128,1024]{3,2,1,0:T(8,128)(2,1)} %param.4, bf16[48,24,128]{2,1,0:T(8,128)(2,1)S(1)} %bitcast.249), kind=kOutput, calls=%fused_computation.100 | convolution fusion | flops 301989888 | bytes 5275648 | tf_op jit(solution)/shard_map/hwi,io->hwo/dot_general | solution.py:11
  76.6 0.0 slice-start.1
  76.6 0.0 slice-start.3
  76.6 4.0 %fusion.142 = f32[48,24,1024]{2,1,0:T(8,128)} fusion(bf16[3,3,128,1024]{3,2,1,0:T(8,128)(2,1)} %param.4, bf16[48,24,128]{2,1,0:T(8,128)(2,1)S(1)} %bitcast.250), kind=kOutput, calls=%fused_computation.97 | convolution fusion | flops 301989888 | bytes 5275648 | tf_op jit(solution)/shard_map/hwi,io->hwo/dot_general | solution.py:11
  80.6 3.9 %fusion.133 = f32[48,24,1024]{2,1,0:T(8,128)} fusion(bf16[3,3,128,1024]{3,2,1,0:T(8,128)(2,1)} %param.4, bf16[1,48,24,128]{3,2,1,0:T(8,128)(2,1)S(1)} %copy-done.1), kind=kOutput, calls=%fused_computation.88 | convolution fusion | flops 301989888 | bytes 5275648 | tf_op jit(solution)/shard_map/hwi,io->hwo/dot_general | solution.py:11
  84.6 0.0 slice-done
  84.6 0.0 slice-done.2
  84.6 0.0 slice-done.1
  84.6 0.0 slice-done.3
  84.6 13.1 %add_add_fusion = f32[48,24,1024]{2,1,0:T(8,128)} fusion(f32[48,24,1024]{2,1,0:T(8,128)S(1)} %bitcast.253, f32[48,24,1024]{2,1,0:T(8,128)S(1)} %bitcast.255, f32[48,24,1024]{2,1,0:T(8,128)} %fusion.130, f32[48,24,1024]{2,1,0:T(8,128)} %fusion.133, f32[48,24,1024]{2,1,0:T(8,128)} %fusion.136, f32[48,24,1024]{2,1,0:T(8,128)} %fusion.139, ...), kind=kOutput, calls=%fused_computation | convolution fusion | flops 311427072 | bytes 43024384 | tf_op jit(solution)/shard_map/hwi,io->hwo/dot_general | solution.py:11
  97.7 0.0 reduce-scatter.2.cloned.1.call-update
  97.7 1.7 fusion.34
  99.5 0.1 dynamic_update_slice.27
  99.6 2.6 fusion.36
  102.1 6.3 %dynamic_update_slice.28 = f32[50,26,128]{2,1,0:T(8,128)S(1)} dynamic-update-slice(f32[50,26,128]{2,1,0:T(8,128)S(1)} %dynamic_update_slice.27, f32[48,24,128]{2,1,0:T(8,128)} %fusion.36, s32[]{:T(128)} %constant.5.clone.1, s32[]{:T(128)} %constant.6.clone.1, s32[]{:T(128)} %constant.5.clone.1) | dynamic-update-slice | bytes 1179652 | tf_op jit(solution)/shard_map/dynamic_update_slice | solution.py:47
  108.5 2.6 fusion.39
  111.0 6.3 %dynamic_update_slice.29 = f32[50,26,128]{2,1,0:T(8,128)S(1)} dynamic-update-slice(f32[50,26,128]{2,1,0:T(8,128)S(1)} %dynamic_update_slice.28, f32[48,24,128]{2,1,0:T(8,128)} %fusion.39, s32[]{:T(128)} %constant.5.clone.1, s32[]{:T(128)} %constant.7.clone.1, s32[]{:T(128)} %constant.5.clone.1) | dynamic-update-slice | bytes 1179652 | tf_op jit(solution)/shard_map/dynamic_update_slice | solution.py:47
  117.3 1.9 fusion.45
  119.2 2.6 fusion.48
  121.8 6.3 %dynamic_update_slice.31 = f32[50,26,128]{2,1,0:T(8,128)S(1)} dynamic-update-slice(f32[50,26,128]{2,1,0:T(8,128)S(1)} %fusion.45, f32[48,24,128]{2,1,0:T(8,128)} %fusion.48, s32[]{:T(128)} %constant.6.clone.1, s32[]{:T(128)} %constant.6.clone.1, s32[]{:T(128)} %constant.5.clone.1) | dynamic-update-slice | bytes 1179652 | tf_op jit(solution)/shard_map/dynamic_update_slice | solution.py:47
  128.1 2.6 fusion.51
  130.6 6.3 %dynamic_update_slice.32 = f32[50,26,128]{2,1,0:T(8,128)S(1)} dynamic-update-slice(f32[50,26,128]{2,1,0:T(8,128)S(1)} %dynamic_update_slice.31, f32[48,24,128]{2,1,0:T(8,128)} %fusion.51, s32[]{:T(128)} %constant.6.clone.1, s32[]{:T(128)} %constant.7.clone.1, s32[]{:T(128)} %constant.5.clone.1) | dynamic-update-slice | bytes 1179652 | tf_op jit(solution)/shard_map/dynamic_update_slice | solution.py:47
  136.9 1.8 fusion.57
  138.8 2.6 fusion.60
  141.3 6.2 %dynamic_update_slice.34 = f32[50,26,128]{2,1,0:T(8,128)S(1)} dynamic-update-slice(f32[50,26,128]{2,1,0:T(8,128)S(1)} %fusion.57, f32[48,24,128]{2,1,0:T(8,128)} %fusion.60, s32[]{:T(128)} %constant.7.clone.1, s32[]{:T(128)} %constant.6.clone.1, s32[]{:T(128)} %constant.5.clone.1) | dynamic-update-slice | bytes 1179652 | tf_op jit(solution)/shard_map/dynamic_update_slice | solution.py:47
  147.6 2.6 fusion.63
  150.1 6.2 %dynamic_update_slice.35 = f32[50,26,128]{2,1,0:T(8,128)S(1)} dynamic-update-slice(f32[50,26,128]{2,1,0:T(8,128)S(1)} %dynamic_update_slice.34, f32[48,24,128]{2,1,0:T(8,128)} %fusion.63, s32[]{:T(128)} %constant.7.clone.1, s32[]{:T(128)} %constant.7.clone.1, s32[]{:T(128)} %constant.5.clone.1) | dynamic-update-slice | bytes 1179652 | tf_op jit(solution)/shard_map/dynamic_update_slice | solution.py:47
  156.4 0.8 fusion.120
  157.1 40.0 %all-reduce.4.cloned.1.call-done = f32[1024,3,3,128]{3,0,2,1:T(8,128)} async-done(((f32[1024,3,3,128]{3,0,2,1:T(8,128)}), f32[1024,3,3,128]{3,0,2,1:T(8,128)}) %all-reduce.4.cloned.1.call-update) | async-done | bytes 4718608 | tf_op jit(solution)/shard_map/psum | solution.py:61
  197.2 1.6 dynamic-slice_multiply_fusion
  198.8 61.2 %reduce-scatter.2.cloned.1.call-done = f32[6,24,1024]{2,1,0:T(8,128)} async-done(((f32[48,24,1024]{2,1,0:T(8,128)}), f32[6,24,1024]{2,1,0:T(8,128)}) %reduce-scatter.2.cloned.1.call-update) | async-done | bytes 589840 | tf_op jit(solution)/shard_map/reduce_scatter | solution.py:29
  259.9 1.8 convert_bitcast_fusion
  (2 shorter events, 0.0 us)
Async XLA Ops:
  7.2 45.1 %all-gather.2.cloned.1.call-start = ((), (), s32[]{:S(2)}) async-start(), calls=%async_computation.2 | async-start | bytes 2654208 | tf_op jit(solution)/shard_map/all_gather | solution.py:38
  7.9 189.3 %all-reduce.4.cloned.1.call-start = ((), (), s32[]{:S(2)}) async-start(), calls=%async_computation.3 | async-start | bytes 9437184 | tf_op jit(solution)/shard_map/psum | solution.py:61
  7.9 4.1 %copy-start.1 = (bf16[1,48,24,128]{3,2,1,0:T(8,128)(2,1)S(1)}, bf16[1,48,24,128]{3,2,1,0:T(8,128)(2,1)}, u32[]{:S(2)}) copy-start(bf16[1,48,24,128]{3,2,1,0:T(8,128)(2,1)} %param.3) | copy-start | bytes 884740
  52.3 3.2 %copy-start = (bf16[1,48,24,1024]{3,2,0,1:T(8,128)(2,1)S(1)}, bf16[1,48,24,1024]{3,2,0,1:T(8,128)(2,1)}, u32[]{:S(2)}) copy-start(bf16[1,48,24,1024]{3,2,0,1:T(8,128)(2,1)} %all-gather.2.cloned.1.call-done) | copy-start | bytes 7077892
  72.3 187.6 %reduce-scatter.2.cloned.1.call-start = ((), (), s32[]{:S(2)}) async-start(), calls=%async_computation.1 | async-start | bytes 5308416 | tf_op jit(solution)/shard_map/reduce_scatter | solution.py:29
  72.4 12.2 %slice-start = ((s8[4718592]{0:T(1024)(128)(4,1)}), s8[4194304]{0:T(1024)(128)(4,1)S(1)}, s32[]{:S(2)}) async-start(s8[4718592]{0:T(1024)(128)(4,1)} %bitcast.252), calls=%async_computation.4 | async-start | bytes 8388608
  72.4 12.2 %slice-start.2 = ((s8[4718592]{0:T(1024)(128)(4,1)}), s8[4194304]{0:T(1024)(128)(4,1)S(1)}, s32[]{:S(2)}) async-start(s8[4718592]{0:T(1024)(128)(4,1)} %bitcast.254), calls=%async_computation.6 | async-start | bytes 8388608
  76.6 8.0 %slice-start.1 = ((s8[4718592]{0:T(1024)(128)(4,1)}), s8[524288]{0:T(1024)(128)(4,1)S(1)}, s32[]{:S(2)}) async-start(s8[4718592]{0:T(1024)(128)(4,1)} %bitcast.252), calls=%async_computation.5 | async-start | bytes 1048576
  76.6 8.0 %slice-start.3 = ((s8[4718592]{0:T(1024)(128)(4,1)}), s8[524288]{0:T(1024)(128)(4,1)S(1)}, s32[]{:S(2)}) async-start(s8[4718592]{0:T(1024)(128)(4,1)} %bitcast.254), calls=%async_computation.7 | async-start | bytes 1048576
Sparse Core Ops, SparseCore 0:
  9.8 42.4 all-gather.1
  72.5 124.6 all-reduce.3
  199.9 59.9 reduce-scatter.1
where the time goes:
time: 270 us; the launch traced here: 268 us
  waiting for transfers between devices  127 us (47%)
  matrix products  79.7 us (30%)
  local copies, waits for them, and re-layouts  44.6 us (17%)
  between operations  13.9 us (5%)
  other arithmetic  3.4 us (1%)
    reduce_scatter x1, waiting for transfers between devices, on_device(): lax.psum_scatter(conv_rows(xpad, kernel, my_rows * lax.axis_size('filter'...  61.2 us
    dot_general x9, matrix products, conv_rows(): jnp.einsum('hwi,io->hwo', xpad[a:a + count, b:b + width], weights[a, b],...  44.8 us
    psum x1, waiting for transfers between devices, on_device(): whole = lax.psum(grads, 'dp')  40 us
    dynamic_update_slice x7, local copies, waits for them, and re-layouts, on_device(): lax.dynamic_update_slice(back_pad, region + contrib, (start + a, b, 0))  37.7 us
    all_gather x1, waiting for transfers between devices, on_device(): grad_rows = lax.all_gather(cotangent, 'filter', axis=1, tiled=True)[0]  24.7 us
    dot_general x9, matrix products, on_device(): jnp.einsum('hwo,io->hwi', grad_rows, kernel[a, b], preferred_element_type...  20.9 us
    dot_general x9, matrix products, on_device(): jnp.einsum('hwi,hwo->oi', xpad[a:a + count, b:b + width], grad_rows, pref...  14 us
    reshape x1, local copies, waits for them, and re-layouts, on_device(): grads = jnp.stack(taps, 1).reshape(channels, 3, 3, local_in)  6.04 us
  transfers between devices with their start and end apart: 3, of which 3 were waited for; matrix products, arithmetic and copies ran while one was open for 39% of the time, Pallas kernels for 0%

commit v1 on v0

--- a/solution.py
+++ b/solution.py
@@ -35,7 +35,9 @@
     outputs = summed.astype(jnp.bfloat16)[None]
     start = jnp.int32(0)
     back_pad = jnp.zeros((height + 2, width + 2, local_in), jnp.float32)
-    grad_rows = lax.all_gather(cotangent, "filter", axis=1, tiled=True)[0]
+    grad_rows = jnp.concatenate(
+        lax.all_to_all(jnp.stack([cotangent] * lax.axis_size("filter")), "filter", 0, 0), axis=1
+    )[0]
     count = grad_rows.shape[0]
     taps = []
     for a in range(3):

time: 270 us -> 227 us (0.84)
  waiting for transfers between devices: 127 us -> 72.2 us
  starting transfers between devices: 0.12 us -> 9.23 us
    reduce_scatter x1, waiting for transfers between devices: 61.2 us -> 0.01 us  [on_device(): lax.psum_scatter(conv_rows(xpad, kernel, my_rows * lax.axis_size('filter'...]
    all_to_all x0 -> x1, waiting for transfers between devices: none -> 37.8 us  [on_device(): lax.all_to_all(jnp.stack([cotangent] * lax.axis_size('filter')), 'filter'...]
    all_gather x1 -> x0, waiting for transfers between devices: 24.7 us -> none  [on_device(): grad_rows = lax.all_gather(cotangent, 'filter', axis=1, tiled=True)[0]]
    all_to_all x0 -> x1, starting transfers between devices: none -> 9.15 us  [on_device(): lax.all_to_all(jnp.stack([cotangent] * lax.axis_size('filter')), 'filter'...]
    psum x1, waiting for transfers between devices: 40 us -> 34.4 us  [on_device(): whole = lax.psum(grads, 'dp')]
    another operation x0 -> x1, local copies, waits for them, and re-layouts: none -> 2.71 us  [on_device(): jnp.stack([cotangent] * lax.axis_size('filter'))]
  transfers between devices with their start and end apart: 3 -> 3, of which waited for: 3 -> 2; matrix products, arithmetic and copies ran while one was open for 39% -> 47% of each run, Pallas kernels for 0% -> 0%
where the time goes in v1:
time: 227 us; the launch traced here: 226 us
  matrix products  77.8 us (34%)
  waiting for transfers between devices  72.2 us (32%)
  local copies, waits for them, and re-layouts  47.3 us (21%)
  between operations  15.6 us (7%)
  starting transfers between devices  9.23 us (4%)
  other arithmetic  3.4 us (1%)
    dot_general x9, matrix products, conv_rows(): jnp.einsum('hwi,io->hwo', xpad[a:a + count, b:b + width], weights[a, b],...  44.7 us
    all_to_all x1, waiting for transfers between devices, on_device(): lax.all_to_all(jnp.stack([cotangent] * lax.axis_size('filter')), 'filter'...  37.8 us
    dynamic_update_slice x7, local copies, waits for them, and re-layouts, on_device(): lax.dynamic_update_slice(back_pad, region + contrib, (start + a, b, 0))  37.8 us
    psum x1, waiting for transfers between devices, on_device(): whole = lax.psum(grads, 'dp')  34.4 us
    dot_general x9, matrix products, on_device(): jnp.einsum('hwo,io->hwi', grad_rows, kernel[a, b], preferred_element_type...  20.9 us
    dot_general x9, matrix products, on_device(): jnp.einsum('hwi,hwo->oi', xpad[a:a + count, b:b + width], grad_rows, pref...  12.2 us
    all_to_all x1, starting transfers between devices, on_device(): lax.all_to_all(jnp.stack([cotangent] * lax.axis_size('filter')), 'filter'...  9.15 us
    reshape x1, local copies, waits for them, and re-layouts, on_device(): grads = jnp.stack(taps, 1).reshape(channels, 3, 3, local_in)  6.03 us
  transfers between devices with their start and end apart: 3, of which 2 were waited for; matrix products, arithmetic and copies ran while one was open for 47% of the time, Pallas kernels for 0%

profile of v1, /device:TPU:1, one launch (start us, length us, event | category | flops | bytes accessed | tf_op | source)
XLA Modules:
  0.0 225.6 jit_solution(15523568246439427183)
XLA Ops:
  8.0 2.7 %stack.41 = bf16[8,1,6,24,1024]{4,3,2,1,0:T(8,128)(2,1)} broadcast(bf16[6,24,1024]{2,1,0:T(8,128)(2,1)} %bitcast.200), dimensions={2,3,4} | broadcast | bytes 2654208 | tf_op jit(solution)/shard_map/stack | solution.py:39
  10.7 0.0 copy-start
  10.7 9.1 %all-to-all-start = ((bf16[8,1,6,24,1024]{4,3,2,1,0:T(8,128)(2,1)}), bf16[8,1,6,24,1024]{4,3,2,1,0:T(8,128)(2,1)S(1)}, u32[]{:S(2)}, u32[]{:S(2)}) async-start(bf16[8,1,6,24,1024]{4,3,2,1,0:T(8,128)(2,1)} %stack.41), calls=%async_computation.1 | async-start | bytes 4718592 | tf_op jit(solution)/shard_map/all_to_all | solution.py:39
  19.9 0.0 all-reduce.4.cloned.1.call-start
  19.9 0.0 copy-done
  19.9 3.9 %fusion.15 = f32[48,24,1024]{2,1,0:T(8,128)} fusion(bf16[3,3,128,1024]{3,2,1,0:T(8,128)(2,1)} %param.4, bf16[48,24,128]{2,1,0:T(8,128)(2,1)S(1)} %bitcast.180), kind=kOutput, calls=%fused_computation.43 | convolution fusion | flops 301989888 | bytes 5275648 | tf_op jit(solution)/shard_map/hwi,io->hwo/dot_general | solution.py:11
  23.8 3.8 %fusion.18 = f32[48,24,1024]{2,1,0:T(8,128)} fusion(bf16[3,3,128,1024]{3,2,1,0:T(8,128)(2,1)} %param.4, bf16[48,24,128]{2,1,0:T(8,128)(2,1)S(1)} %bitcast.181), kind=kOutput, calls=%fused_computation.46 | convolution fusion | flops 301989888 | bytes 5275648 | tf_op jit(solution)/shard_map/hwi,io->hwo/dot_general | solution.py:11
  27.7 3.9 %fusion.21 = f32[48,24,1024]{2,1,0:T(8,128)} fusion(bf16[3,3,128,1024]{3,2,1,0:T(8,128)(2,1)} %param.4, bf16[48,24,128]{2,1,0:T(8,128)(2,1)S(1)} %bitcast.182), kind=kOutput, calls=%fused_computation.49 | convolution fusion | flops 301989888 | bytes 5275648 | tf_op jit(solution)/shard_map/hwi,io->hwo/dot_general | solution.py:11
  31.6 3.8 %fusion.27 = f32[48,24,1024]{2,1,0:T(8,128)} fusion(bf16[3,3,128,1024]{3,2,1,0:T(8,128)(2,1)} %param.4, bf16[48,24,128]{2,1,0:T(8,128)(2,1)S(1)} %bitcast.183), kind=kOutput, calls=%fused_computation.55 | convolution fusion | flops 301989888 | bytes 5275648 | tf_op jit(solution)/shard_map/hwi,io->hwo/dot_general | solution.py:11
  35.4 3.9 %fusion.30 = f32[48,24,1024]{2,1,0:T(8,128)} fusion(bf16[3,3,128,1024]{3,2,1,0:T(8,128)(2,1)} %param.4, bf16[48,24,128]{2,1,0:T(8,128)(2,1)S(1)} %bitcast.184), kind=kOutput, calls=%fused_computation.58 | convolution fusion | flops 301989888 | bytes 5275648 | tf_op jit(solution)/shard_map/hwi,io->hwo/dot_general | solution.py:11
  39.3 37.8 %all-to-all-done = bf16[8,1,6,24,1024]{4,3,2,1,0:T(8,128)(2,1)S(1)} async-done(((bf16[8,1,6,24,1024]{4,3,2,1,0:T(8,128)(2,1)}), bf16[8,1,6,24,1024]{4,3,2,1,0:T(8,128)(2,1)S(1)}, u32[]{:S(2)}, u32[]{:S(2)}) %all-to-all-start) | async-done | bytes 2359328 | tf_op jit(solution)/shard_map/all_to_all | solution.py:39
  77.2 1.4 fusion.10
  78.5 1.4 fusion.9
  79.9 1.4 fusion.8
  81.2 1.4 fusion.7
  82.6 1.4 fusion.6
  84.0 1.3 fusion.5
  85.3 1.3 fusion.4
  86.6 1.3 fusion.3
  88.0 1.4 fusion.2
  89.3 6.0 %copy.45 = f32[1024,3,3,128]{3,0,2,1:T(8,128)} copy(f32[1024,3,3,128]{0,3,2,1:T(8,128)} %bitcast.58) | data formatting | bytes 9437184 | tf_op jit(solution)/shard_map/reshape | solution.py:58
  95.4 0.0 all-reduce.4.cloned.1.call-update
  95.4 0.0 reduce-scatter.2.cloned.1.call-start
  95.4 0.0 slice-start
  95.5 0.0 slice-start.2
  95.5 4.2 %fusion.37 = f32[48,24,1024]{2,1,0:T(8,128)} fusion(bf16[3,3,128,1024]{3,2,1,0:T(8,128)(2,1)} %param.4, bf16[48,24,128]{2,1,0:T(8,128)(2,1)S(1)} %bitcast.193), kind=kOutput, calls=%fused_computation.65 | convolution fusion | flops 301989888 | bytes 5275648 | tf_op jit(solution)/shard_map/hwi,io->hwo/dot_general | solution.py:11
  99.7 0.0 slice-start.1
  99.7 0.0 slice-start.3
  99.7 4.0 %fusion.33 = f32[48,24,1024]{2,1,0:T(8,128)} fusion(bf16[3,3,128,1024]{3,2,1,0:T(8,128)(2,1)} %param.4, bf16[48,24,128]{2,1,0:T(8,128)(2,1)S(1)} %bitcast.194), kind=kOutput, calls=%fused_computation.61 | convolution fusion | flops 301989888 | bytes 5275648 | tf_op jit(solution)/shard_map/hwi,io->hwo/dot_general | solution.py:11
  103.7 3.9 %fusion.24 = f32[48,24,1024]{2,1,0:T(8,128)} fusion(bf16[3,3,128,1024]{3,2,1,0:T(8,128)(2,1)} %param.4, bf16[1,48,24,128]{3,2,1,0:T(8,128)(2,1)S(1)} %copy-done), kind=kOutput, calls=%fused_computation.52 | convolution fusion | flops 301989888 | bytes 5275648 | tf_op jit(solution)/shard_map/hwi,io->hwo/dot_general | solution.py:11
  107.6 0.0 slice-done
  107.6 0.0 slice-done.2
  107.6 0.0 slice-done.1
  107.6 0.0 slice-done.3
  107.7 13.1 %add_add_fusion = f32[48,24,1024]{2,1,0:T(8,128)} fusion(f32[48,24,1024]{2,1,0:T(8,128)S(1)} %bitcast.197, f32[48,24,1024]{2,1,0:T(8,128)S(1)} %bitcast.199, f32[48,24,1024]{2,1,0:T(8,128)} %fusion.21, f32[48,24,1024]{2,1,0:T(8,128)} %fusion.24, f32[48,24,1024]{2,1,0:T(8,128)} %fusion.27, f32[48,24,1024]{2,1,0:T(8,128)} %fusion.30, ...), kind=kOutput, calls=%fused_computation | convolution fusion | flops 311427072 | bytes 43024384 | tf_op jit(solution)/shard_map/hwi,io->hwo/dot_general | solution.py:11
  120.8 0.0 reduce-scatter.2.cloned.1.call-update
  120.8 1.7 fusion.35
  122.6 0.1 dynamic_update_slice.27
  122.7 2.6 %convolution_add_fusion.7 = f32[48,24,128]{2,1,0:T(8,128)} fusion(bf16[48,24,1024]{2,1,0:T(8,128)(2,1)S(1)} %bitcast.172, bf16[3,3,128,1024]{3,2,1,0:T(8,128)(2,1)} %param.4, f32[48,24,128]{2,1,0:T(8,128)S(1)} %fusion.35), kind=kOutput, calls=%fused_computation.10 | convolution fusion | flops 302137344 | bytes 3801088 | tf_op jit(solution)/shard_map/hwo,io->hwi/dot_general | solution.py:45
  125.2 6.4 %dynamic_update_slice.28 = f32[50,26,128]{2,1,0:T(8,128)S(1)} dynamic-update-slice(f32[50,26,128]{2,1,0:T(8,128)S(1)} %dynamic_update_slice.27, f32[48,24,128]{2,1,0:T(8,128)} %convolution_add_fusion.7, s32[]{:T(128)} %constant.5.clone.1, s32[]{:T(128)} %constant.6.clone.1, s32[]{:T(128)} %constant.5.clone.1) | dynamic-update-slice | bytes 1179652 | tf_op jit(solution)/shard_map/dynamic_update_slice | solution.py:49
  131.6 2.6 %convolution_add_fusion.6 = f32[48,24,128]{2,1,0:T(8,128)} fusion(bf16[48,24,1024]{2,1,0:T(8,128)(2,1)S(1)} %bitcast.173, f32[50,26,128]{2,1,0:T(8,128)S(1)} %dynamic_update_slice.28, bf16[3,3,128,1024]{3,2,1,0:T(8,128)(2,1)} %param.4), kind=kOutput, calls=%fused_computation.9 | convolution fusion | flops 302137344 | bytes 3801088 | tf_op jit(solution)/shard_map/hwo,io->hwi/dot_general | solution.py:45
  134.2 6.3 %dynamic_update_slice.29 = f32[50,26,128]{2,1,0:T(8,128)S(1)} dynamic-update-slice(f32[50,26,128]{2,1,0:T(8,128)S(1)} %dynamic_update_slice.28, f32[48,24,128]{2,1,0:T(8,128)} %convolution_add_fusion.6, s32[]{:T(128)} %constant.5.clone.1, s32[]{:T(128)} %constant.7.clone.1, s32[]{:T(128)} %constant.5.clone.1) | dynamic-update-slice | bytes 1179652 | tf_op jit(solution)/shard_map/dynamic_update_slice | solution.py:49
  140.5 1.9 fusion.1
  142.4 2.6 %convolution_add_fusion.4 = f32[48,24,128]{2,1,0:T(8,128)} fusion(bf16[48,24,1024]{2,1,0:T(8,128)(2,1)S(1)} %bitcast.175, f32[50,26,128]{2,1,0:T(8,128)S(1)} %fusion.1, bf16[3,3,128,1024]{3,2,1,0:T(8,128)(2,1)} %param.4), kind=kOutput, calls=%fused_computation.6 | convolution fusion | flops 302137344 | bytes 3801088 | tf_op jit(solution)/shard_map/hwo,io->hwi/dot_general | solution.py:45
  145.0 6.3 %dynamic_update_slice.31 = f32[50,26,128]{2,1,0:T(8,128)S(1)} dynamic-update-slice(f32[50,26,128]{2,1,0:T(8,128)S(1)} %fusion.1, f32[48,24,128]{2,1,0:T(8,128)} %convolution_add_fusion.4, s32[]{:T(128)} %constant.6.clone.1, s32[]{:T(128)} %constant.6.clone.1, s32[]{:T(128)} %constant.5.clone.1) | dynamic-update-slice | bytes 1179652 | tf_op jit(solution)/shard_map/dynamic_update_slice | solution.py:49
  151.2 2.6 %convolution_add_fusion.3 = f32[48,24,128]{2,1,0:T(8,128)} fusion(bf16[48,24,1024]{2,1,0:T(8,128)(2,1)S(1)} %bitcast.176, f32[50,26,128]{2,1,0:T(8,128)S(1)} %dynamic_update_slice.31, bf16[3,3,128,1024]{3,2,1,0:T(8,128)(2,1)} %param.4), kind=kOutput, calls=%fused_computation.5 | convolution fusion | flops 302137344 | bytes 3801088 | tf_op jit(solution)/shard_map/hwo,io->hwi/dot_general | solution.py:45
  153.8 6.3 %dynamic_update_slice.32 = f32[50,26,128]{2,1,0:T(8,128)S(1)} dynamic-update-slice(f32[50,26,128]{2,1,0:T(8,128)S(1)} %dynamic_update_slice.31, f32[48,24,128]{2,1,0:T(8,128)} %convolution_add_fusion.3, s32[]{:T(128)} %constant.6.clone.1, s32[]{:T(128)} %constant.7.clone.1, s32[]{:T(128)} %constant.5.clone.1) | dynamic-update-slice | bytes 1179652 | tf_op jit(solution)/shard_map/dynamic_update_slice | solution.py:49
  160.1 1.9 fusion
  162.0 2.6 %convolution_add_fusion.1 = f32[48,24,128]{2,1,0:T(8,128)} fusion(bf16[48,24,1024]{2,1,0:T(8,128)(2,1)S(1)} %bitcast.178, f32[50,26,128]{2,1,0:T(8,128)S(1)} %fusion, bf16[3,3,128,1024]{3,2,1,0:T(8,128)(2,1)} %param.4), kind=kOutput, calls=%fused_computation.2 | convolution fusion | flops 302137344 | bytes 3801088 | tf_op jit(solution)/shard_map/hwo,io->hwi/dot_general | solution.py:45
  164.5 6.2 %dynamic_update_slice.34 = f32[50,26,128]{2,1,0:T(8,128)S(1)} dynamic-update-slice(f32[50,26,128]{2,1,0:T(8,128)S(1)} %fusion, f32[48,24,128]{2,1,0:T(8,128)} %convolution_add_fusion.1, s32[]{:T(128)} %constant.7.clone.1, s32[]{:T(128)} %constant.6.clone.1, s32[]{:T(128)} %constant.5.clone.1) | dynamic-update-slice | bytes 1179652 | tf_op jit(solution)/shard_map/dynamic_update_slice | solution.py:49
  170.8 2.6 %convolution_add_fusion = f32[48,24,128]{2,1,0:T(8,128)} fusion(bf16[48,24,1024]{2,1,0:T(8,128)(2,1)S(1)} %bitcast.179, f32[50,26,128]{2,1,0:T(8,128)S(1)} %dynamic_update_slice.34, bf16[3,3,128,1024]{3,2,1,0:T(8,128)(2,1)} %param.4), kind=kOutput, calls=%fused_computation.1 | convolution fusion | flops 302137344 | bytes 3801088 | tf_op jit(solution)/shard_map/hwo,io->hwi/dot_general | solution.py:45
  173.3 6.2 %dynamic_update_slice.35 = f32[50,26,128]{2,1,0:T(8,128)S(1)} dynamic-update-slice(f32[50,26,128]{2,1,0:T(8,128)S(1)} %dynamic_update_slice.34, f32[48,24,128]{2,1,0:T(8,128)} %convolution_add_fusion, s32[]{:T(128)} %constant.7.clone.1, s32[]{:T(128)} %constant.7.clone.1, s32[]{:T(128)} %constant.5.clone.1) | dynamic-update-slice | bytes 1179652 | tf_op jit(solution)/shard_map/dynamic_update_slice | solution.py:49
  179.6 0.8 fusion.11
  180.4 34.4 %all-reduce.4.cloned.1.call-done = f32[1024,3,3,128]{3,0,2,1:T(8,128)} async-done(((f32[1024,3,3,128]{3,0,2,1:T(8,128)}), f32[1024,3,3,128]{3,0,2,1:T(8,128)}) %all-reduce.4.cloned.1.call-update) | async-done | bytes 4718608 | tf_op jit(solution)/shard_map/psum | solution.py:63
  214.7 1.6 dynamic-slice_multiply_fusion
  216.3 0.0 reduce-scatter.2.cloned.1.call-done
  216.3 1.8 convert_bitcast_fusion
  (2 shorter events, 0.0 us)
Async XLA Ops:
  10.7 9.2 %copy-start = (bf16[1,48,24,128]{3,2,1,0:T(8,128)(2,1)S(1)}, bf16[1,48,24,128]{3,2,1,0:T(8,128)(2,1)}, u32[]{:S(2)}) copy-start(bf16[1,48,24,128]{3,2,1,0:T(8,128)(2,1)} %param.3) | copy-start | bytes 884740
  10.7 66.4 %all-to-all-start = ((bf16[8,1,6,24,1024]{4,3,2,1,0:T(8,128)(2,1)}), bf16[8,1,6,24,1024]{4,3,2,1,0:T(8,128)(2,1)S(1)}, u32[]{:S(2)}, u32[]{:S(2)}) async-start(bf16[8,1,6,24,1024]{4,3,2,1,0:T(8,128)(2,1)} %stack.41), calls=%async_computation.1 | async-start | bytes 4718592 | tf_op jit(solution)/shard_map/all_to_all | solution.py:39
  19.9 194.9 %all-reduce.4.cloned.1.call-start = ((), (), s32[]{:S(2)}) async-start(), calls=%async_computation.3 | async-start | bytes 9437184 | tf_op jit(solution)/shard_map/psum | solution.py:63
  95.4 120.9 %reduce-scatter.2.cloned.1.call-start = ((), (), s32[]{:S(2)}) async-start(), calls=%async_computation.2 | async-start | bytes 5308416 | tf_op jit(solution)/shard_map/reduce_scatter | solution.py:29
  95.4 12.2 %slice-start = ((s8[4718592]{0:T(1024)(128)(4,1)}), s8[4194304]{0:T(1024)(128)(4,1)S(1)}, s32[]{:S(2)}) async-start(s8[4718592]{0:T(1024)(128)(4,1)} %bitcast.196), calls=%async_computation.4 | async-start | bytes 8388608
  95.5 12.2 %slice-start.2 = ((s8[4718592]{0:T(1024)(128)(4,1)}), s8[4194304]{0:T(1024)(128)(4,1)S(1)}, s32[]{:S(2)}) async-start(s8[4718592]{0:T(1024)(128)(4,1)} %bitcast.198), calls=%async_computation.6 | async-start | bytes 8388608
  99.7 8.0 %slice-start.1 = ((s8[4718592]{0:T(1024)(128)(4,1)}), s8[524288]{0:T(1024)(128)(4,1)S(1)}, s32[]{:S(2)}) async-start(s8[4718592]{0:T(1024)(128)(4,1)} %bitcast.196), calls=%async_computation.5 | async-start | bytes 1048576
  99.7 8.0 %slice-start.3 = ((s8[4718592]{0:T(1024)(128)(4,1)}), s8[524288]{0:T(1024)(128)(4,1)S(1)}, s32[]{:S(2)}) async-start(s8[4718592]{0:T(1024)(128)(4,1)} %bitcast.198), calls=%async_computation.7 | async-start | bytes 1048576
Sparse Core Ops, SparseCore 0:
  95.5 119.1 all-reduce.3
Sparse Core Ops, SparseCore 1:
  120.9 56.5 reduce-scatter.1
